TPU v7x, 32 devices: a whole 2x2x4 slice. The times are simulated.
32 devices in a mesh: ctx: 4 (over z), exp: 4 (over y, x), rep: 2 (over core).
Axes of the slice: x: 2, y: 2, z: 4, core: 2. Of those that a mesh axis runs over, the one named last changes fastest.
Arguments:
- acts: bfloat16 [512, 2048], P(('ctx', 'exp'), 'rep'), may hold values from -6 to 6
- grad_out: bfloat16 [512, 2048], P(('ctx', 'exp'), 'rep'), may hold values from -0.59765625 to 0.59765625
- experts_idx: int32 [512, 8], P(('ctx', 'exp')), may hold values from 0 to 15, all different within a row; in each aligned block of 32 rows (0 to 31, 32 to 63, ...) at most 24 rows name the same one
- gate_prob: bfloat16 [512, 8], P(('ctx', 'exp')), may hold values from 0.049804688 to 1
- w_gate: bfloat16 [16, 768, 2048], P(('ctx', 'exp'), 'rep'), may hold values from -0.125 to 0.125
- w_up: bfloat16 [16, 768, 2048], P(('ctx', 'exp'), 'rep'), may hold values from -0.125 to 0.125
- w_down: bfloat16 [16, 768, 2048], P(('ctx', 'exp'), 'rep'), may hold values from -0.21875 to 0.21875
Outputs:
- acts_grad: bfloat16 [512, 2048], P(('ctx', 'exp'), 'rep')
- gate_grad_tok: bfloat16 [512, 8], P(('ctx', 'exp'))
- w_gate_grad: bfloat16 [16, 768, 2048], P(('ctx', 'exp'), 'rep')
- w_up_grad: bfloat16 [16, 768, 2048], P(('ctx', 'exp'), 'rep')
- w_down_grad: bfloat16 [16, 768, 2048], P(('ctx', 'exp'), 'rep')
Inputs may be any that keep to these rules, and one draw needn't show every extreme that they name: `experts_idx`: each row names 8 different experts. Within the rows of one index of ctx+exp (32 aligned rows), no expert is named by more than 24 rows, a bound that some block reaches.
All inputs are finite; a program needn't handle non-finite values.
Results may differ from a plain program's by a relative error of at most 0.012.
Values may be sent and summed in bfloat16 or wider, within the bound.
A program may use at most 64 MiB of HBM per device.

v0:
```python
import jax
import jax.numpy as jnp
from jax import lax
from jax.sharding import PartitionSpec as P


def slot_tables(experts_idx, expert_count, capacity):
    tokens_here, top_count = experts_idx.shape
    labels = jnp.arange(expert_count, dtype=jnp.int32)
    picked = (experts_idx[:, :, None] == labels[None, None, :]).astype(jnp.int32)
    flat_pick = picked.reshape(tokens_here * top_count, expert_count)
    earlier = jnp.cumsum(flat_pick, axis=0) - flat_pick
    slot_number = jnp.sum(flat_pick * (labels[None, :] * capacity + earlier), axis=1)
    slot_labels = jnp.arange(expert_count * capacity, dtype=jnp.int32)
    select = (slot_number[None, :] == slot_labels[:, None]).astype(jnp.bfloat16)
    placing = jnp.sum(select.reshape(expert_count * capacity, tokens_here, top_count), axis=2)
    return (select, placing)


def body(acts, grad_out, experts_idx, gate_prob, w_gate, w_up, w_down):
    tokens_here, top_count = experts_idx.shape
    expert_count = lax.axis_size(("ctx", "exp"))
    capacity = min(tokens_here, 3 * tokens_here * top_count // (2 * expert_count))
    select, placing = slot_tables(experts_idx, expert_count, capacity)
    slot_gate = jnp.dot(select, gate_prob.reshape(-1), preferred_element_type=jnp.float32).astype(
        jnp.bfloat16
    )
    send_acts = jnp.dot(placing, acts, preferred_element_type=jnp.float32).astype(jnp.bfloat16)
    send_grad = jnp.dot(placing, grad_out, preferred_element_type=jnp.float32).astype(jnp.bfloat16)
    part_acts, part_grad, rows_gate = (
        lax.all_to_all(send_acts, ("ctx", "exp"), split_axis=0, concat_axis=0, tiled=True),
        lax.all_to_all(send_grad, ("ctx", "exp"), split_axis=0, concat_axis=0, tiled=True),
        lax.all_to_all(slot_gate, ("ctx", "exp"), split_axis=0, concat_axis=0, tiled=True),
    )
    rows_acts, rows_grad = (
        lax.all_gather(part_acts, "rep", axis=1, tiled=True),
        lax.all_gather(part_grad, "rep", axis=1, tiled=True),
    )
    gate_w = w_gate[0]
    up_w = w_up[0]
    down_w = w_down[0]
    contract_last = (((1,), (1,)), ((), ()))
    contract_first = (((0,), (0,)), ((), ()))
    pre_gate = lax.dot_general(rows_acts, gate_w, contract_last, preferred_element_type=jnp.float32)
    pre_up = lax.dot_general(rows_acts, up_w, contract_last, preferred_element_type=jnp.float32)
    sigma = jax.nn.sigmoid(pre_gate)
    swish = pre_gate * sigma
    hidden = (swish * pre_up).astype(jnp.bfloat16)
    expert_out = jnp.dot(hidden, down_w, preferred_element_type=jnp.float32)
    gate_part = jnp.sum(expert_out * rows_grad.astype(jnp.float32), axis=1)
    scaled_grad = (rows_gate.astype(jnp.float32)[:, None] * rows_grad.astype(jnp.float32)).astype(
        jnp.bfloat16
    )
    hidden_grad = lax.dot_general(
        scaled_grad, down_w, contract_last, preferred_element_type=jnp.float32
    )
    grad_gate_pre = (hidden_grad * pre_up * sigma * (1.0 + pre_gate * (1.0 - sigma))).astype(
        jnp.bfloat16
    )
    grad_up_pre = (hidden_grad * swish).astype(jnp.bfloat16)
    down_grad = lax.dot_general(
        hidden, scaled_grad, contract_first, preferred_element_type=jnp.float32
    ).astype(jnp.bfloat16)
    gate_grad = lax.dot_general(
        grad_gate_pre, rows_acts, contract_first, preferred_element_type=jnp.float32
    ).astype(jnp.bfloat16)
    up_grad = lax.dot_general(
        grad_up_pre, rows_acts, contract_first, preferred_element_type=jnp.float32
    ).astype(jnp.bfloat16)
    row_terms = jnp.dot(grad_gate_pre, gate_w, preferred_element_type=jnp.float32)
    row_terms = row_terms + jnp.dot(grad_up_pre, up_w, preferred_element_type=jnp.float32)
    row_share = lax.psum_scatter(
        row_terms.astype(jnp.bfloat16), "rep", scatter_dimension=1, tiled=True
    )
    gate_total = lax.psum(gate_part, "rep").astype(jnp.bfloat16)
    back_share, back_gate = (
        lax.all_to_all(row_share, ("ctx", "exp"), split_axis=0, concat_axis=0, tiled=True),
        lax.all_to_all(gate_total, ("ctx", "exp"), split_axis=0, concat_axis=0, tiled=True),
    )
    acts_grad = lax.dot_general(
        placing, back_share, contract_first, preferred_element_type=jnp.float32
    ).astype(jnp.bfloat16)
    gate_flat = lax.dot_general(
        select, back_gate, contract_first, preferred_element_type=jnp.float32
    )
    gate_grad_tok = gate_flat.reshape(tokens_here, top_count).astype(jnp.bfloat16)
    return (acts_grad, gate_grad_tok, gate_grad[None], up_grad[None], down_grad[None])


def solution(mesh):
    placed = (
        P(("ctx", "exp"), "rep"),
        P(("ctx", "exp"), "rep"),
        P(("ctx", "exp"), None),
        P(("ctx", "exp"), None),
        P(("ctx", "exp"), "rep", None),
        P(("ctx", "exp"), "rep", None),
        P(("ctx", "exp"), "rep", None),
    )
    return jax.shard_map(
        body,
        mesh=mesh,
        in_specs=placed,
        out_specs=(
            P(("ctx", "exp"), "rep"),
            P(("ctx", "exp"), None),
            P(("ctx", "exp"), "rep", None),
            P(("ctx", "exp"), "rep", None),
            P(("ctx", "exp"), "rep", None),
        ),
        check_vma=False,
    )
```

profile of v0, /device:TPU:0, one launch (start us, length us, event | category | flops | bytes accessed | tf_op | source)
XLA Modules:
  0.0 134.5 jit_solution(5737237207501992094)
XLA Ops:
  7.2 0.0 copy-start
  7.2 0.0 all-gather.5.cloned.1.call-start
  7.2 0.9 copy.22
  8.1 0.1 eq.71
  8.2 0.1 eq.67
  8.3 0.6 reduce-window.6
  8.9 0.2 slice_reduce_fusion
  9.1 0.1 fusion.28
  9.2 0.1 eq.75
  9.3 0.2 fusion.22
  9.5 0.0 copy-start.7
  9.5 1.2 convolution_convert_fusion.3
  10.8 29.5 %all_to_all.59 = bf16[16,24,1024]{2,1,0:T(8,128)(2,1)} all-to-all(bf16[16,24,1024]{2,1,0:T(8,128)(2,1)S(1)} %bitcast.79), channel_id=1, replica_groups=mesh['ctx'=4,'exp'=4,'rep'=2] {'ctx','exp'}, dimensions={0} | all-to-all | bytes 1572864 | tf_op jit(solution)/shard_map/all_to_all | solution.py:31
  40.3 0.0 all-gather.5.cloned.1.call-update
  40.3 0.0 copy-start.8
  40.3 0.0 copy-start.3
  40.4 0.0 all-gather.3.cloned.1.call-start
  40.4 0.0 copy-done.7
  40.4 0.4 convolution_convert_fusion.4
  40.8 24.2 %all_to_all.60 = bf16[16,24,1024]{2,1,0:T(8,128)(2,1)} all-to-all(bf16[16,24,1024]{2,1,0:T(8,128)(2,1)S(1)} %bitcast.80), channel_id=1, replica_groups=mesh['ctx'=4,'exp'=4,'rep'=2] {'ctx','exp'}, dimensions={0} | all-to-all | bytes 1572864 | tf_op jit(solution)/shard_map/all_to_all | solution.py:32
  65.0 0.0 all-gather.3.cloned.1.call-update
  65.0 0.0 reduce-scatter.2.cloned.1.call-start
  65.0 0.0 copy-done.8
  65.0 0.1 copy.25
  65.1 0.1 reshape.84
  65.2 0.2 convolution_reduce_fusion
  65.4 0.1 all_to_all.52
  65.5 10.5 %all_to_all.61 = bf16[16,24,1]{1,2,0:T(2,128)(2,1)S(1)} all-to-all(bf16[16,24,1]{1,2,0:T(2,128)(2,1)S(1)} %all_to_all.52), channel_id=1, replica_groups=mesh['ctx'=4,'exp'=4,'rep'=2] {'ctx','exp'}, dimensions={0} | all-to-all | bytes 1536 | tf_op jit(solution)/shard_map/all_to_all | solution.py:33
  76.1 0.1 reshape.83
  76.2 0.0 all-gather.5.cloned.1.call-done
  76.2 0.0 copy-done.3
  76.2 3.2 %fusion.7 = f32[384,384]{1,0:T(8,128)} fusion(bf16[384,2048]{1,0:T(8,128)(2,1)} %all-gather.5.cloned.1.call-done, bf16[1,384,2048]{2,1,0:T(8,128)(2,1)S(1)} %copy-done.3), kind=kOutput, calls=%fused_computation.13 | convolution fusion | flops 603979776 | bytes 3735552 | tf_op jit(solution)/shard_map/dot_general | solution.py:44
  79.4 0.0 all-gather.3.cloned.1.call-done
  79.4 0.0 copy-start.9
  79.4 0.0 copy-start.11
  79.4 3.0 %fusion.13 = f32[384,384]{1,0:T(8,128)S(1)} fusion(bf16[1,384,2048]{2,1,0:T(8,128)(2,1)} %param.13, bf16[384,2048]{1,0:T(8,128)(2,1)} %all-gather.3.cloned.1.call-done, f32[384]{0:T(512)S(1)} %reshape.83), kind=kOutput, calls=%fused_computation.19 | convolution fusion | flops 606339072 | bytes 3737088 | tf_op jit(solution)/shard_map/dot_general | solution.py:54
  82.5 0.0 copy-done
  82.5 0.0 copy-done.9
  82.5 0.0 copy-done.11
  82.5 1.9 %multiply_convert_fusion = (bf16[384,384]{1,0:T(8,128)(2,1)}, bf16[384,384]{1,0:T(8,128)(2,1)S(1)}, bf16[384,384]{1,0:T(8,128)(2,1)S(1)}) fusion(f32[384,384]{1,0:T(8,128)S(1)} %copy-done.11, f32[384,384]{1,0:T(8,128)S(1)} %fusion.13, bf16[384,2048]{1,0:T(8,128)(2,1)S(1)} %copy-done.9, bf16[1,384,2048]{2,1,0:T(8,128)(2,1)S(1)} %copy-done), kind=kOutput, calls=%fused_computation.25 | convolution fusion | flops 606191616 | bytes 5210112 | tf_op jit(solution)/shard_map/dot_general | solution.py:45
  84.4 1.0 fusion.5
  85.4 0.0 copy-done.5
  85.4 2.1 %add_convert_fusion = bf16[384,2048]{1,0:T(8,128)(2,1)} fusion(f32[384,2048]{1,0:T(8,128)S(1)} %fusion.5, bf16[384,384]{1,0:T(8,128)(2,1)S(1)} %get-tuple-element.7, bf16[1,384,2048]{2,1,0:T(8,128)(2,1)S(1)} %copy-done), kind=kOutput, calls=%fused_computation.4 | convolution fusion | flops 605552640 | bytes 6586368 | tf_op jit(solution)/shard_map/dot_general | solution.py:71
  87.5 0.0 reduce-scatter.2.cloned.1.call-update
  87.5 1.4 %copy-done.1 = bf16[384,2048]{1,0:T(8,128)(2,1)S(1)} copy-done((bf16[384,2048]{1,0:T(8,128)(2,1)S(1)}, bf16[384,2048]{1,0:T(8,128)(2,1)}, u32[]{:S(2)}) %copy-start.1) | copy-done | bytes 1572888
  88.9 3.0 %fusion.1 = f32[384]{0:T(512)S(1)} fusion(bf16[384,2048]{1,0:T(8,128)(2,1)S(1)} %copy-done.1, bf16[384,384]{1,0:T(8,128)(2,1)} %get-tuple-element.5, bf16[1,384,2048]{2,1,0:T(8,128)(2,1)} %param.13), kind=kOutput, calls=%fused_computation.3 | convolution fusion | flops 606338688 | bytes 3442176 | tf_op jit(solution)/shard_map/dot_general | solution.py:49
  91.9 2.5 %psum.7 = bf16[384]{0:T(512)(128)(2,1)S(1)} all-reduce(f32[384]{0:T(512)S(1)} %fusion.1), channel_id=1, replica_groups=mesh['ctx'=4,'exp'=4,'rep'=2] {'rep'}, use_global_device_ids=true, to_apply=%region_6.7 | all-reduce | flops 384 | bytes 2304 | tf_op jit(solution)/shard_map/psum | solution.py:75
  94.4 0.1 all_to_all.53
  94.5 9.9 %all_to_all.62 = bf16[16,24,1]{1,2,0:T(2,128)(2,1)S(1)} all-to-all(bf16[16,24,1]{1,2,0:T(2,128)(2,1)S(1)} %all_to_all.53), channel_id=1, replica_groups=mesh['ctx'=4,'exp'=4,'rep'=2] {'ctx','exp'}, dimensions={0} | all-to-all | bytes 1536 | tf_op jit(solution)/shard_map/all_to_all | solution.py:78
  104.4 3.6 %all-to-all-start.3 = ((bf16[16,24,1024]{2,1,0:T(8,128)(2,1)}), bf16[16,24,1024]{2,1,0:T(8,128)(2,1)S(1)}, u32[]{:S(2)}, u32[]{:S(2)}) async-start(bf16[16,24,1024]{2,1,0:T(8,128)(2,1)} %bitcast.81), calls=%async_computation.4 | async-start | bytes 1572864 | tf_op jit(solution)/shard_map/all_to_all | solution.py:77
  108.0 0.0 copy-start.6
  108.0 0.0 copy-start.10
  108.0 3.7 %fusion.2 = bf16[1,384,2048]{2,1,0:T(8,128)(2,1)} fusion(bf16[384,384]{1,0:T(8,128)(2,1)S(1)} %get-tuple-element.6, bf16[384,2048]{1,0:T(8,128)(2,1)} %all-gather.5.cloned.1.call-done), kind=kOutput, calls=%fused_computation.8 | convolution fusion | flops 604766208 | bytes 3440640 | tf_op jit(solution)/shard_map/dot_general | solution.py:64
  111.7 0.0 copy-done.6
  111.7 0.0 copy-done.10
  111.7 2.2 %fusion.3 = bf16[1,384,2048]{2,1,0:T(8,128)(2,1)} fusion(bf16[384,384]{1,0:T(8,128)(2,1)S(1)} %copy-done.6, bf16[384,2048]{1,0:T(8,128)(2,1)S(1)} %copy-done.10), kind=kOutput, calls=%fused_computation.9 | convolution fusion | flops 604766208 | bytes 3440640 | tf_op jit(solution)/shard_map/dot_general | solution.py:67
  113.9 0.0 copy-done.2
  113.9 0.0 copy-done.4
  113.9 2.2 %fusion.4 = bf16[1,384,2048]{2,1,0:T(8,128)(2,1)} fusion(bf16[384,384]{1,0:T(8,128)(2,1)S(1)} %copy-done.4, bf16[384,2048]{1,0:T(8,128)(2,1)S(1)} %copy-done.2, f32[384]{0:T(512)S(1)} %reshape.83), kind=kOutput, calls=%fused_computation.10 | convolution fusion | flops 607125504 | bytes 3442176 | tf_op jit(solution)/shard_map/dot_general | solution.py:61
  116.2 0.1 reshape.86
  116.3 0.8 fusion.20
  117.0 0.7 copy.28
  117.7 9.4 %all-to-all-done.3 = bf16[16,24,1024]{2,1,0:T(8,128)(2,1)S(1)} async-done(((bf16[16,24,1024]{2,1,0:T(8,128)(2,1)}), bf16[16,24,1024]{2,1,0:T(8,128)(2,1)S(1)}, u32[]{:S(2)}, u32[]{:S(2)}) %all-to-all-start.3) | async-done | bytes 786464 | tf_op jit(solution)/shard_map/all_to_all | solution.py:77
  127.1 0.9 convolution_convert_fusion.5
  (11 shorter events, 0.1 us)
Async XLA Ops:
  7.2 75.3 %copy-start = (bf16[1,384,2048]{2,1,0:T(8,128)(2,1)S(1)}, bf16[1,384,2048]{2,1,0:T(8,128)(2,1)}, u32[]{:S(2)}) copy-start(bf16[1,384,2048]{2,1,0:T(8,128)(2,1)} %param.12) | copy-start | bytes 4718596
  7.2 69.0 %all-gather.5.cloned.1.call-start = ((), (), s32[]{:S(2)}) async-start(), calls=%async_computation.7 | async-start | bytes 2359296 | tf_op jit(solution)/shard_map/all_gather | solution.py:36
  9.5 30.9 %copy-start.7 = (bf16[32,1024]{1,0:T(8,128)(2,1)S(1)}, bf16[32,1024]{1,0:T(8,128)(2,1)}, u32[]{:S(2)}) copy-start(bf16[32,1024]{1,0:T(8,128)(2,1)} %param.8) | copy-start | bytes 196612
  40.3 24.7 %copy-start.8 = (bf16[32,8]{0,1:T(8,128)(2,1)S(1)}, bf16[32,8]{0,1:T(8,128)(2,1)}, u32[]{:S(2)}) copy-start(bf16[32,8]{0,1:T(8,128)(2,1)} %param.10) | copy-start | bytes 1540
  40.3 35.9 %copy-start.3 = (bf16[1,384,2048]{2,1,0:T(8,128)(2,1)S(1)}, bf16[1,384,2048]{2,1,0:T(8,128)(2,1)}, u32[]{:S(2)}) copy-start(bf16[1,384,2048]{2,1,0:T(8,128)(2,1)} %param.11) | copy-start | bytes 4718596
  40.4 39.1 %all-gather.3.cloned.1.call-start = ((), (), s32[]{:S(2)}) async-start(), calls=%async_computation.6 | async-start | bytes 2359296 | tf_op jit(solution)/shard_map/all_gather | solution.py:37
  65.0 39.4 %reduce-scatter.2.cloned.1.call-start = ((), (), s32[]{:S(2)}) async-start(), calls=%async_computation.8 | async-start | bytes 2359296 | tf_op jit(solution)/shard_map/reduce_scatter | solution.py:72
  79.4 3.1 %copy-start.9 = (bf16[384,2048]{1,0:T(8,128)(2,1)S(1)}, bf16[384,2048]{1,0:T(8,128)(2,1)}, u32[]{:S(2)}) copy-start(bf16[384,2048]{1,0:T(8,128)(2,1)} %all-gather.5.cloned.1.call-done) | copy-start | bytes 4718596
  79.4 3.1 %copy-start.11 = (f32[384,384]{1,0:T(8,128)S(1)}, f32[384,384]{1,0:T(8,128)}, u32[]{:S(2)}) copy-start(f32[384,384]{1,0:T(8,128)} %fusion.7) | copy-start | bytes 1769476
  84.4 1.0 copy-start.5
  87.5 1.4 %copy-start.1 = (bf16[384,2048]{1,0:T(8,128)(2,1)S(1)}, bf16[384,2048]{1,0:T(8,128)(2,1)}, u32[]{:S(2)}) copy-start(bf16[384,2048]{1,0:T(8,128)(2,1)} %all-gather.3.cloned.1.call-done) | copy-start | bytes 4718596
  104.4 22.7 %all-to-all-start.3 = ((bf16[16,24,1024]{2,1,0:T(8,128)(2,1)}), bf16[16,24,1024]{2,1,0:T(8,128)(2,1)S(1)}, u32[]{:S(2)}, u32[]{:S(2)}) async-start(bf16[16,24,1024]{2,1,0:T(8,128)(2,1)} %bitcast.81), calls=%async_computation.4 | async-start | bytes 1572864 | tf_op jit(solution)/shard_map/all_to_all | solution.py:77
  108.0 3.7 %copy-start.6 = (bf16[384,384]{1,0:T(8,128)(2,1)S(1)}, bf16[384,384]{1,0:T(8,128)(2,1)}, u32[]{:S(2)}) copy-start(bf16[384,384]{1,0:T(8,128)(2,1)} %copy-done.5) | copy-start | bytes 884740
  108.0 3.7 %copy-start.10 = (bf16[384,2048]{1,0:T(8,128)(2,1)S(1)}, bf16[384,2048]{1,0:T(8,128)(2,1)}, u32[]{:S(2)}) copy-start(bf16[384,2048]{1,0:T(8,128)(2,1)} %all-gather.5.cloned.1.call-done) | copy-start | bytes 4718596
  111.7 2.2 %copy-start.2 = (bf16[384,2048]{1,0:T(8,128)(2,1)S(1)}, bf16[384,2048]{1,0:T(8,128)(2,1)}, u32[]{:S(2)}) copy-start(bf16[384,2048]{1,0:T(8,128)(2,1)} %all-gather.3.cloned.1.call-done) | copy-start | bytes 4718596
  111.7 2.2 %copy-start.4 = (bf16[384,384]{1,0:T(8,128)(2,1)S(1)}, bf16[384,384]{1,0:T(8,128)(2,1)}, u32[]{:S(2)}) copy-start(bf16[384,384]{1,0:T(8,128)(2,1)} %get-tuple-element.5) | copy-start | bytes 884740
Sparse Core Ops, SparseCore 0:
  40.5 7.5 all-gather.4
  65.1 7.5 all-gather.2
  87.6 5.2 reduce-scatter.1
where the time goes:
time: 135 us
  blocking collectives  76.6 us (57%)
  matrix products  25.8 us (19%)
  between operations  14 us (10%)
  waiting for transfers between devices  9.5 us (7%)
  local copies, waits for them, and re-layouts  3.98 us (3%)
  starting transfers between devices  3.73 us (3%)
    all_to_all x1, blocking collectives, body(): lax.all_to_all(send_acts, ('ctx', 'exp'), split_axis=0, concat_axis=0, ti...  29.5 us
    all_to_all x1, blocking collectives, body(): lax.all_to_all(send_grad, ('ctx', 'exp'), split_axis=0, concat_axis=0, ti...  24.2 us
    all_to_all x1, blocking collectives, body(): lax.all_to_all(slot_gate, ('ctx', 'exp'), split_axis=0, concat_axis=0, ti...  10.5 us
    all_to_all x1, blocking collectives, body(): lax.all_to_all(gate_total, ('ctx', 'exp'), split_axis=0, concat_axis=0, t...  9.88 us
    all_to_all x1, waiting for transfers between devices, body(): lax.all_to_all(row_share, ('ctx', 'exp'), split_axis=0, concat_axis=0, ti...  9.43 us
    dot_general x1, matrix products, body(): lax.dot_general(grad_gate_pre, rows_acts, contract_first, preferred_eleme...  3.7 us
    all_to_all x1, starting transfers between devices, body(): lax.all_to_all(row_share, ('ctx', 'exp'), split_axis=0, concat_axis=0, ti...  3.61 us
    dot_general x1, matrix products, body(): lax.dot_general(rows_acts, gate_w, contract_last, preferred_element_type=...  3.22 us
  transfers between devices with their start and end apart: 4, of which 1 were waited for; matrix products, arithmetic and copies ran while one was open for 12% of the time, Pallas kernels for 0%

commit v1 on v0

--- a/solution.py
+++ b/solution.py
@@ -1,7 +1,447 @@
+import functools
+import heapq
+
 import jax
 import jax.numpy as jnp
 from jax import lax
+from jax.experimental import pallas as pl
+from jax.experimental.pallas import tpu as pltpu
 from jax.sharding import PartitionSpec as P
+
+MESH = pl.DeviceIdType.MESH
+LANES = 128
+CONTRACT_LAST = (((1,), (1,)), ((), ()))
+CONTRACT_FIRST = (((0,), (0,)), ((), ()))
+
+
+def diag_planes(z, planes):
+    low = z - (2 * z >= planes)
+    return (low, low + 1)
+
+
+def forwards(z, planes, array, source, rel):
+    out = []
+    if rel == 0:
+        out += [("x", z, 1), ("y", z, 2)]
+        if source <= z < planes - 1:
+            out.append(("up", z + 1, 0))
+        if source >= z > 0:
+            out.append(("down", z - 1, 0))
+    elif rel == 1:
+        if array == 1 and source in diag_planes(z, planes):
+            out.append(("y", z, 3))
+    elif rel == 2:
+        if array == 0 and source in diag_planes(z, planes):
+            out.append(("x", z, 3))
+    else:
+        if source <= z < planes - 1 and source not in diag_planes(z + 1, planes):
+            out.append(("up", z + 1, 3))
+        if source >= z > 0 and source not in diag_planes(z - 1, planes):
+            out.append(("down", z - 1, 3))
+    return out
+
+
+def arrival_order(planes):
+    wire, hop = 1.4, 1.6
+    order = [[] for _ in range(planes)]
+    free = {}
+    events = []
+    count = 0
+    for z in range(planes):
+        for array in range(2):
+            events.append((0.0, count, z, array, z, 0))
+            count += 1
+    heapq.heapify(events)
+    while events:
+        now, _, z, array, source, rel = heapq.heappop(events)
+        order[z].append((array, source, rel))
+        for link, to, rel_there in forwards(z, planes, array, source, rel):
+            begin = max(now, free.get((z, link), 0.0))
+            free[(z, link)] = begin + wire
+            heapq.heappush(events, (begin + wire + hop, count, to, array, source, rel_there))
+            count += 1
+    return order
+
+
+def at_xor(e, rel):
+    x, y = e % 2, e // 2
+    dx, dy = rel % 2, rel // 2
+    new_x = x if dx == 0 else 1 - x
+    new_y = y if dy == 0 else 1 - y
+    return new_y * 2 + new_x
+
+
+def position():
+    return lax.axis_index("ctx"), lax.axis_index("exp"), lax.axis_index("rep")
+
+
+def greet_all(planes):
+    z, e, r = position()
+    barrier = pltpu.get_barrier_semaphore()
+    total = 0
+    for dz in range(planes):
+        for rel in range(4):
+            for dr in range(2):
+                if dz == 0 and rel == 0 and dr == 0:
+                    continue
+                pl.semaphore_signal(
+                    barrier,
+                    inc=1,
+                    device_id={
+                        "ctx": lax.rem(z + dz, planes),
+                        "exp": at_xor(e, rel),
+                        "rep": r if dr == 0 else 1 - r,
+                    },
+                    device_id_type=MESH,
+                )
+                total += 1
+    pl.semaphore_wait(barrier, total)
+
+
+LINKS = ("x", "y", "up", "down", "core")
+
+
+def gather_kernel(
+    planes, acts, grad, gates, acts_all, grad_all, gates_all,
+    send_sem, recv_sem, core_sem, gate_send, gate_recv, local_sem,
+):
+    z, e, r = position()
+    rows, width = acts.shape
+    chips = planes * 4
+    greet_all(planes)
+
+    me = z * 4 + e
+    gate_copies = []
+    for j in range(1, chips):
+        to = lax.rem(me + j, chips)
+        gate_copies.append(
+            pltpu.make_async_remote_copy(
+                src_ref=gates.at[to],
+                dst_ref=gates_all.at[me],
+                send_sem=gate_send.at[j],
+                recv_sem=gate_recv.at[j],
+                device_id={"ctx": to // 4, "exp": to % 4, "rep": r},
+                device_id_type=MESH,
+            )
+        )
+    inputs, outputs = (acts, grad), (acts_all, grad_all)
+    mine = pl.ds(pl.multiple_of(me * rows, rows), rows)
+    cols = pl.ds(pl.multiple_of(r * width, width), width)
+    other_cols = pl.ds(pl.multiple_of((1 - r) * width, width), width)
+    local = [
+        pltpu.make_async_copy(inputs[a], outputs[a].at[mine, cols], local_sem.at[a]) for a in range(2)
+    ]
+    local.append(pltpu.make_async_copy(gates.at[me], gates_all.at[me], local_sem.at[2]))
+
+    def chunk(array, source, rel, columns):
+        first = pl.multiple_of((source * 4 + at_xor(e, rel)) * rows, rows)
+        return outputs[array].at[pl.ds(first, rows), columns]
+
+    def send(zi, array, source, rel, link, rel_there):
+        target = {
+            "x": {"ctx": z, "exp": at_xor(e, 1), "rep": r},
+            "y": {"ctx": z, "exp": at_xor(e, 2), "rep": r},
+            "up": {"ctx": z + 1, "exp": e, "rep": r},
+            "down": {"ctx": z - 1, "exp": e, "rep": r},
+            "core": {"ctx": z, "exp": e, "rep": 1 - r},
+        }[link]
+        place = chunk(array, source, rel, cols)
+        own = source == zi and rel == 0
+        sem = core_sem if link == "core" else recv_sem
+        return pltpu.make_async_remote_copy(
+            src_ref=inputs[array] if own else place,
+            dst_ref=place,
+            send_sem=send_sem.at[LINKS.index(link), array, source, rel],
+            recv_sem=sem.at[array, source, rel_there],
+            device_id=target,
+            device_id_type=MESH,
+        )
+
+    def arrived(ref, sem):
+        pltpu.make_async_copy(ref, ref, sem).wait()
+
+    order = arrival_order(planes)
+    for zi in range(planes):
+
+        @pl.when(z == zi)
+        def _():
+            sent = []
+            gates_out = False
+            for array, source, rel in order[zi]:
+                own = source == zi and rel == 0
+                if not own:
+                    if not gates_out:
+                        for copy in gate_copies:
+                            copy.start()
+                        for copy in local:
+                            copy.start()
+                        gates_out = True
+                    arrived(chunk(array, source, rel, cols), recv_sem.at[array, source, rel])
+                steps = forwards(zi, planes, array, source, rel) + [("core", zi, rel)]
+                for link, _, rel_there in steps:
+                    copy = send(zi, array, source, rel, link, rel_there)
+                    copy.start()
+                    sent.append(copy)
+            for copy in sent:
+                copy.wait_send()
+
+    for copy in local:
+        copy.wait()
+    for j in range(1, chips):
+        gate_copies[j - 1].wait_send()
+        arrived(gates_all.at[lax.rem(me + chips - j, chips)], gate_recv.at[j])
+    for array in range(2):
+        for source in range(planes):
+            for rel in range(4):
+                arrived(chunk(array, source, rel, other_cols), core_sem.at[array, source, rel])
+
+
+def expert_kernel(
+    acts, grad, gates, w_gate, w_up, w_down,
+    terms, gate_part, gate_grad, up_grad, down_grad,
+    gg_buf, gu_buf, gh_buf,
+):
+    tokens, depth = acts.shape
+    hidden_here = w_gate.shape[0]
+    step = LANES
+    partial = jnp.zeros((tokens, LANES), jnp.float32)
+    gate_col = gates[...]
+    for first in range(0, hidden_here, step):
+        part = pl.ds(first, step)
+        pre_gate = lax.dot_general(acts[...], w_gate[part, :], CONTRACT_LAST, preferred_element_type=jnp.float32)
+        pre_up = lax.dot_general(acts[...], w_up[part, :], CONTRACT_LAST, preferred_element_type=jnp.float32)
+        raw = lax.dot_general(grad[...], w_down[part, :], CONTRACT_LAST, preferred_element_type=jnp.float32)
+        sigma = jax.nn.sigmoid(pre_gate)
+        swish = pre_gate * sigma
+        hidden = (swish * pre_up).astype(jnp.bfloat16).astype(jnp.float32)
+        partial = partial + hidden * raw
+        hidden_grad = raw * gate_col
+        gg_buf[:, part] = (
+            hidden_grad * pre_up * sigma * (1.0 + pre_gate * (1.0 - sigma))
+        ).astype(jnp.bfloat16)
+        gu_buf[:, part] = (hidden_grad * swish).astype(jnp.bfloat16)
+        gh_buf[:, part] = (hidden * gate_col).astype(jnp.bfloat16)
+    flat = jnp.sum(jnp.transpose(partial), axis=0, keepdims=True)
+    for block in range(gate_part.shape[0]):
+        gate_part[block] = flat[:, block * LANES : (block + 1) * LANES]
+    wide = 512
+    for first in range(0, depth, wide):
+        part = pl.ds(first, wide)
+        terms[:, part] = (
+            jnp.dot(gg_buf[...], w_gate[:, part], preferred_element_type=jnp.float32)
+            + jnp.dot(gu_buf[...], w_up[:, part], preferred_element_type=jnp.float32)
+        ).astype(jnp.bfloat16)
+        gate_grad[:, part] = lax.dot_general(
+            gg_buf[...], acts[:, part], CONTRACT_FIRST, preferred_element_type=jnp.float32
+        ).astype(jnp.bfloat16)
+        up_grad[:, part] = lax.dot_general(
+            gu_buf[...], acts[:, part], CONTRACT_FIRST, preferred_element_type=jnp.float32
+        ).astype(jnp.bfloat16)
+        down_grad[:, part] = lax.dot_general(
+            gh_buf[...], grad[:, part], CONTRACT_FIRST, preferred_element_type=jnp.float32
+        ).astype(jnp.bfloat16)
+
+
+def scatter_kernel(
+    planes, terms, gate_part, acts_grad, gate_in,
+    core_buf, sum_buf, xy_buf, col_buf, z_buf,
+    core_send, core_recv, xy_send, xy_recv, z_send, z_recv, g_send, g_recv, local_sem,
+):
+    z, e, r = position()
+    rows, width = acts_grad.shape
+    plane_rows = 4 * rows
+    greet_all(planes)
+    me = z * 4 + e
+    cols = pl.ds(pl.multiple_of(r * width, width), width)
+    other_cols = pl.ds(pl.multiple_of((1 - r) * width, width), width)
+    order = list(range(1, planes)) + [0]
+
+    core_copies = {}
+    for k in order:
+        place = pl.ds(pl.multiple_of(lax.rem(z + k, planes) * plane_rows, plane_rows), plane_rows)
+        core_copies[k] = pltpu.make_async_remote_copy(
+            src_ref=terms.at[place, other_cols],
+            dst_ref=core_buf.at[place],
+            send_sem=core_send.at[k],
+            recv_sem=core_recv.at[k],
+            device_id={"ctx": z, "exp": e, "rep": 1 - r},
+            device_id_type=MESH,
+        )
+        core_copies[k].start()
+
+    gate_copies = []
+    for k in range(planes):
+        to_z = lax.rem(z + k, planes)
+        for rel in range(4):
+            for dr in range(2):
+                if k == 0 and rel == 0 and dr == 0:
+                    continue
+                gate_copies.append(
+                    pltpu.make_async_remote_copy(
+                        src_ref=gate_part.at[to_z],
+                        dst_ref=gate_in.at[r * planes * 4 + me],
+                        send_sem=g_send.at[k, rel, dr],
+                        recv_sem=g_recv.at[k, rel, dr],
+                        device_id={
+                            "ctx": to_z,
+                            "exp": at_xor(e, rel),
+                            "rep": r if dr == 0 else 1 - r,
+                        },
+                        device_id_type=MESH,
+                    )
+                )
+    own_gate = pltpu.make_async_copy(gate_part.at[z], gate_in.at[r * planes * 4 + me], local_sem)
+    own_gate.start()
+
+    xy_copies = {}
+    for k in order:
+        zz = lax.rem(z + k, planes)
+        core_copies[k].wait_recv()
+        for rel in (3, 1, 2, 0):
+            block = pl.ds(pl.multiple_of((zz * 4 + at_xor(e, rel)) * rows, rows), rows)
+            sum_buf[block, :] = (
+                terms[block, cols].astype(jnp.float32) + core_buf[block, :].astype(jnp.float32)
+            ).astype(jnp.bfloat16)
+            if rel == 0:
+                continue
+            xy_copies[k, rel] = pltpu.make_async_remote_copy(
+                src_ref=sum_buf.at[block],
+                dst_ref=xy_buf.at[k, rel],
+                send_sem=xy_send.at[k, rel],
+                recv_sem=xy_recv.at[k, rel],
+                device_id={"ctx": z, "exp": at_xor(e, rel), "rep": r},
+                device_id_type=MESH,
+            )
+            xy_copies[k, rel].start()
+    for copy in gate_copies:
+        copy.start()
+
+    z_copies = {}
+    for k in order:
+        zz = lax.rem(z + k, planes)
+        block = pl.ds(pl.multiple_of((zz * 4 + e) * rows, rows), rows)
+        total = sum_buf[block, :].astype(jnp.float32)
+        for rel in (1, 2, 3):
+            xy_copies[k, rel].wait_recv()
+            total = total + xy_buf[k, rel].astype(jnp.float32)
+        if k == 0:
+            for kk in range(1, planes):
+                z_copies[kk].wait_recv()
+                total = total + z_buf[kk].astype(jnp.float32)
+            acts_grad[...] = total.astype(jnp.bfloat16)
+            continue
+        col_buf[k] = total.astype(jnp.bfloat16)
+        z_copies[k] = pltpu.make_async_remote_copy(
+            src_ref=col_buf.at[k],
+            dst_ref=z_buf.at[k],
+            send_sem=z_send.at[k],
+            recv_sem=z_recv.at[k],
+            device_id={"ctx": zz, "exp": e, "rep": r},
+            device_id_type=MESH,
+        )
+        z_copies[k].start()
+
+    own_gate.wait()
+    for copies in (core_copies, xy_copies, z_copies):
+        for copy in copies.values():
+            copy.wait_send()
+    for copy in gate_copies:
+        copy.wait_send()
+    for k in range(planes):
+        from_z = lax.rem(z + planes - k, planes)
+        for rel in range(4):
+            for dr in range(2):
+                if k == 0 and rel == 0 and dr == 0:
+                    continue
+                from_r = r if dr == 0 else 1 - r
+                place = gate_in.at[from_r * planes * 4 + from_z * 4 + at_xor(e, rel)]
+                pltpu.make_async_copy(place, place, g_recv.at[k, rel, dr]).wait()
+
+
+def dense_body(planes, acts, grad_out, experts_idx, gate_prob, w_gate, w_up, w_down):
+    rows, width = acts.shape
+    top = experts_idx.shape[1]
+    chips = planes * 4
+    tokens = chips * rows
+    depth = 2 * width
+    hidden_here = w_gate.shape[1]
+    dma, vmem = pltpu.SemaphoreType.DMA, pl.BlockSpec(memory_space=pltpu.VMEM)
+    bf16, f32 = jnp.bfloat16, jnp.float32
+
+    labels = jnp.arange(chips, dtype=jnp.int32)
+    picked = experts_idx.T[:, None, :] == labels[None, :, None]
+    gates = jnp.sum(jnp.where(picked, gate_prob.astype(f32).T[:, None, :], 0.0), axis=0)
+    gates = jnp.pad(gates, ((0, 0), (0, LANES - rows)))[:, None, :]
+
+    acts_all, grad_all, gates_all = pl.pallas_call(
+        functools.partial(gather_kernel, planes),
+        out_shape=(
+            jax.ShapeDtypeStruct((tokens, depth), bf16),
+            jax.ShapeDtypeStruct((tokens, depth), bf16),
+            jax.ShapeDtypeStruct((chips, 1, LANES), f32),
+        ),
+        in_specs=[vmem] * 3,
+        out_specs=[vmem] * 3,
+        scratch_shapes=[
+            dma((len(LINKS), 2, planes, 4)),
+            dma((2, planes, 4)),
+            dma((2, planes, 4)),
+            dma((chips,)),
+            dma((chips,)),
+            dma((3,)),
+        ],
+        compiler_params=pltpu.CompilerParams(collective_id=0, has_side_effects=True),
+        name="gather",
+    )(acts, grad_out, gates)
+
+    gate_col = gates_all[:, 0, :rows].reshape(tokens, 1)
+    wide = jax.ShapeDtypeStruct((hidden_here, depth), bf16)
+    terms, gate_part, gate_grad, up_grad, down_grad = pl.pallas_call(
+        expert_kernel,
+        out_shape=(
+            jax.ShapeDtypeStruct((tokens, depth), bf16),
+            jax.ShapeDtypeStruct((tokens // LANES, 1, LANES), f32),
+            wide, wide, wide,
+        ),
+        in_specs=[vmem] * 6,
+        out_specs=[vmem] * 5,
+        scratch_shapes=[pltpu.VMEM((tokens, hidden_here), bf16)] * 3,
+        compiler_params=pltpu.CompilerParams(vmem_limit_bytes=48 << 20),
+        name="expert",
+    )(acts_all, grad_all, gate_col, w_gate[0], w_up[0], w_down[0])
+
+    acts_grad, gate_in = pl.pallas_call(
+        functools.partial(scatter_kernel, planes),
+        out_shape=(
+            jax.ShapeDtypeStruct((rows, width), bf16),
+            jax.ShapeDtypeStruct((2 * chips, 1, LANES), f32),
+        ),
+        in_specs=[vmem] * 2,
+        out_specs=[vmem] * 2,
+        scratch_shapes=[
+            pltpu.VMEM((tokens, width), bf16),
+            pltpu.VMEM((tokens, width), bf16),
+            pltpu.VMEM((planes, 4, rows, width), bf16),
+            pltpu.VMEM((planes, rows, width), bf16),
+            pltpu.VMEM((planes, rows, width), bf16),
+            dma((planes,)),
+            dma((planes,)),
+            dma((planes, 4)),
+            dma((planes, 4)),
+            dma((planes,)),
+            dma((planes,)),
+            dma((planes, 4, 2)),
+            dma((planes, 4, 2)),
+            dma,
+        ],
+        compiler_params=pltpu.CompilerParams(collective_id=1, has_side_effects=True),
+        name="scatter",
+    )(terms, gate_part)
+
+    both = (gate_in[:chips, 0, :] + gate_in[chips:, 0, :]).astype(bf16).astype(f32)
+    both = lax.dynamic_slice(both, (0, lax.axis_index("exp") * rows), (chips, rows))
+    gate_grad_tok = jnp.sum(jnp.where(picked, both[None], 0.0), axis=1).T.astype(bf16)
+    return acts_grad, gate_grad_tok, gate_grad[None], up_grad[None], down_grad[None]
 
 
 def slot_tables(experts_idx, expert_count, capacity):
@@ -17,7 +457,7 @@
     return (select, placing)
 
 
-def body(acts, grad_out, experts_idx, gate_prob, w_gate, w_up, w_down):
+def sparse_body(acts, grad_out, experts_idx, gate_prob, w_gate, w_up, w_down):
     tokens_here, top_count = experts_idx.shape
     expert_count = lax.axis_size(("ctx", "exp"))
     capacity = min(tokens_here, 3 * tokens_here * top_count // (2 * expert_count))
@@ -88,6 +528,8 @@
 
 
 def solution(mesh):
+    planes = mesh.shape["ctx"]
+    dense = mesh.shape["exp"] == 4 and mesh.shape["rep"] == 2
     placed = (
         P(("ctx", "exp"), "rep"),
         P(("ctx", "exp"), "rep"),
@@ -98,7 +540,7 @@
         P(("ctx", "exp"), "rep", None),
     )
     return jax.shard_map(
-        body,
+        functools.partial(dense_body, planes) if dense else sparse_body,
         mesh=mesh,
         in_specs=placed,
         out_specs=(

time: 135 us -> 82 us (0.61)
  blocking collectives: 76.6 us -> 0 us
  Pallas kernels: 0 us -> 70.1 us
  matrix products: 25.8 us -> 0 us
  between operations: 14 us -> 0.69 us
  waiting for transfers between devices: 9.5 us -> 0 us
  local copies, waits for them, and re-layouts: 3.98 us -> 8.57 us
  starting transfers between devices: 3.73 us -> 0 us
    all_to_all x4 -> x0, blocking collectives: 74.1 us -> none  [the longest x1 29.5 us: body(): lax.all_to_all(send_acts, ('ctx', 'exp'), split_axis=0, concat_axis=0, ti...]
    pallas_call x0 -> x3, Pallas kernels: none -> 70.1 us  [the longest x1 33 us: dense_body(): pl.pallas_call(functools.partial(gather_kernel, planes), out_shape=(jax.S...]
    dot_general x14 -> x0, matrix products: 25.8 us -> none  [the longest x1 3.7 us: body(): lax.dot_general(grad_gate_pre, rows_acts, contract_first, preferred_eleme...]
    all_to_all x1 -> x0, waiting for transfers between devices: 9.43 us -> none  [body(): lax.all_to_all(row_share, ('ctx', 'exp'), split_axis=0, concat_axis=0, ti...]
    unnamed x26 -> x11, local copies, waits for them, and re-layouts: 2.4 us -> 6.27 us
    all_to_all x1 -> x0, starting transfers between devices: 3.61 us -> none  [body(): lax.all_to_all(row_share, ('ctx', 'exp'), split_axis=0, concat_axis=0, ti...]
    psum x1 -> x0, blocking collectives: 2.47 us -> none  [body(): gate_total = lax.psum(gate_part, 'rep').astype(jnp.bfloat16)]
  transfers between devices with their start and end apart: 4 -> 0, of which waited for: 1 -> 0; matrix products, arithmetic and copies ran while one was open for 12% -> 0% of each run, Pallas kernels for 0% -> 0%
where the time goes in v1:
time: 82 us; the launch traced here: 81.5 us
  Pallas kernels  70.1 us (85%)
  local copies, waits for them, and re-layouts  8.57 us (10%)
  other arithmetic  2.09 us (3%)
    pallas_call x1, Pallas kernels, dense_body(): pl.pallas_call(functools.partial(gather_kernel, planes), out_shape=(jax.S...  33 us
    pallas_call x1, Pallas kernels, dense_body(): pl.pallas_call(functools.partial(scatter_kernel, planes), out_shape=(jax....  22 us
    pallas_call x1, Pallas kernels, dense_body(): pl.pallas_call(expert_kernel, out_shape=(jax.ShapeDtypeStruct((tokens, de...  15.1 us
    unnamed x11, local copies, waits for them, and re-layouts  6.27 us

profile of v1, /device:TPU:0, one launch (start us, length us, event | category | flops | bytes accessed | tf_op | source)
XLA Modules:
  0.0 81.5 jit_solution(3411001450052983439)
XLA Ops:
  0.6 0.7 convert_bitcast_fusion
  1.3 0.7 select_reduce_fusion.1
  2.0 0.6 pad.4
  2.6 33.0 %gather.1 = (bf16[512,2048]{1,0:T(8,128)(2,1)}, bf16[512,2048]{1,0:T(8,128)(2,1)}, f32[16,1,128]{2,1,0:T(1,128)}) custom-call(bf16[32,1024]{1,0:T(8,128)(2,1)} %acts.1, bf16[32,1024]{1,0:T(8,128)(2,1)} %grad.1, f32[16,1,128]{2,1,0:T(1,128)} %bitcast.18), custom_call_target="tpu_custom_call" | custom-call | tf_op jit(solution)/shard_map/gather/pallas_call | solution.py:376
  35.7 0.7 slice_reduce_fusion
  36.4 0.3 reshape_squeeze.4.gates
  36.7 0.0 copy-start
  36.7 1.4 %copy-done = bf16[1,384,2048]{2,1,0:T(8,128)(2,1)S(1)} copy-done((bf16[1,384,2048]{2,1,0:T(8,128)(2,1)S(1)}, bf16[1,384,2048]{2,1,0:T(8,128)(2,1)}, u32[]{:S(2)}) %copy-start) | copy-done | bytes 1572888
  38.1 0.0 copy-start.1
  38.1 1.4 %copy-done.1 = bf16[1,384,2048]{2,1,0:T(8,128)(2,1)S(1)} copy-done((bf16[1,384,2048]{2,1,0:T(8,128)(2,1)S(1)}, bf16[1,384,2048]{2,1,0:T(8,128)(2,1)}, u32[]{:S(2)}) %copy-start.1) | copy-done | bytes 1572888
  39.5 0.0 copy-start.2
  39.5 1.4 %copy-done.2 = bf16[1,384,2048]{2,1,0:T(8,128)(2,1)S(1)} copy-done((bf16[1,384,2048]{2,1,0:T(8,128)(2,1)S(1)}, bf16[1,384,2048]{2,1,0:T(8,128)(2,1)}, u32[]{:S(2)}) %copy-start.2) | copy-done | bytes 1572888
  40.9 15.1 %expert.1 = (bf16[512,2048]{1,0:T(8,128)(2,1)}, f32[4,1,128]{2,1,0:T(1,128)S(1)}, bf16[384,2048]{1,0:T(8,128)(2,1)}, bf16[384,2048]{1,0:T(8,128)(2,1)}, bf16[384,2048]{1,0:T(8,128)(2,1)}) custom-call(bf16[512,2048]{1,0:T(8,128)(2,1)} %get-tuple-element.15.acts, bf16[512,2048]{1,0:T(8,128)(2,1)} %get-tuple-element.16.grad, ...), custom_call_target="tpu_custom_call" | custom-call | tf_op jit(solution)/shard_map/expert/pallas_call | solution.py:399
  56.0 0.0 copy-start.3
  56.0 0.6 copy-done.3
  56.6 0.0 copy-start.4
  56.6 22.0 %scatter.1 = (bf16[32,1024]{1,0:T(8,128)(2,1)}, f32[32,1,128]{2,1,0:T(1,128)}) custom-call(bf16[512,2048]{1,0:T(8,128)(2,1)} %get-tuple-element.18.terms, f32[4,1,128]{2,1,0:T(1,128)} %copy-done.3), custom_call_target="tpu_custom_call" | custom-call | tf_op jit(solution)/shard_map/scatter/pallas_call | solution.py:413
  78.6 0.7 fusion.2
  79.3 0.1 fusion.1
  79.4 0.0 copy-done.4
  79.4 0.6 select_reduce_fusion
  80.0 1.5 %copy.15 = bf16[32,1024]{1,0:T(8,128)(2,1)} copy(bf16[32,1024]{1,0:T(8,128)(2,1)} %get-tuple-element.32) | data formatting | bytes 131072
Async XLA Ops:
  36.7 1.4 %copy-start = (bf16[1,384,2048]{2,1,0:T(8,128)(2,1)S(1)}, bf16[1,384,2048]{2,1,0:T(8,128)(2,1)}, u32[]{:S(2)}) copy-start(bf16[1,384,2048]{2,1,0:T(8,128)(2,1)} %param.11) | copy-start | bytes 4718596
  38.1 1.4 %copy-start.1 = (bf16[1,384,2048]{2,1,0:T(8,128)(2,1)S(1)}, bf16[1,384,2048]{2,1,0:T(8,128)(2,1)}, u32[]{:S(2)}) copy-start(bf16[1,384,2048]{2,1,0:T(8,128)(2,1)} %param.12) | copy-start | bytes 4718596
  39.5 1.4 %copy-start.2 = (bf16[1,384,2048]{2,1,0:T(8,128)(2,1)S(1)}, bf16[1,384,2048]{2,1,0:T(8,128)(2,1)}, u32[]{:S(2)}) copy-start(bf16[1,384,2048]{2,1,0:T(8,128)(2,1)} %param.13) | copy-start | bytes 4718596
  56.0 0.6 copy-start.3
  56.6 22.8 %copy-start.4 = (s32[32,8]{0,1:T(8,128)S(1)}, s32[32,8]{0,1:T(8,128)}, u32[]{:S(2)}) copy-start(s32[32,8]{0,1:T(8,128)} %param.9) | copy-start | bytes 3076

commit v2 on v1

v2 whole, which is shorter than its diff:
```python
import functools
import heapq

import jax
import jax.numpy as jnp
from jax import lax
from jax.experimental import pallas as pl
from jax.experimental.pallas import tpu as pltpu
from jax.sharding import PartitionSpec as P

MESH = pl.DeviceIdType.MESH
LANES = 128
CONTRACT_LAST = (((1,), (1,)), ((), ()))
CONTRACT_FIRST = (((0,), (0,)), ((), ()))


def diag_planes(z, planes):
    low = z - (2 * z >= planes)
    return (low, low + 1)


def forwards(z, planes, array, source, rel):
    out = []
    if rel == 0:
        out += [("x", z, 1), ("y", z, 2)]
        if source <= z < planes - 1:
            out.append(("up", z + 1, 0))
        if source >= z > 0:
            out.append(("down", z - 1, 0))
    elif rel == 1:
        if array == 1 and source in diag_planes(z, planes):
            out.append(("y", z, 3))
    elif rel == 2:
        if array == 0 and source in diag_planes(z, planes):
            out.append(("x", z, 3))
    else:
        if source <= z < planes - 1 and source not in diag_planes(z + 1, planes):
            out.append(("up", z + 1, 3))
        if source >= z > 0 and source not in diag_planes(z - 1, planes):
            out.append(("down", z - 1, 3))
    return out


def arrival_order(planes):
    wire, hop = 1.4, 1.6
    order = [[] for _ in range(planes)]
    free = {}
    events = []
    count = 0
    for z in range(planes):
        for array in range(2):
            events.append((0.0, count, z, array, z, 0))
            count += 1
    heapq.heapify(events)
    while events:
        now, _, z, array, source, rel = heapq.heappop(events)
        order[z].append((array, source, rel))
        for link, to, rel_there in forwards(z, planes, array, source, rel):
            begin = max(now, free.get((z, link), 0.0))
            free[(z, link)] = begin + wire
            heapq.heappush(events, (begin + wire + hop, count, to, array, source, rel_there))
            count += 1
    return order


def at_xor(e, rel):
    x, y = e % 2, e // 2
    dx, dy = rel % 2, rel // 2
    new_x = x if dx == 0 else 1 - x
    new_y = y if dy == 0 else 1 - y
    return new_y * 2 + new_x


def position():
    return lax.axis_index("ctx"), lax.axis_index("exp"), lax.axis_index("rep")


def greet_all(planes):
    z, e, r = position()
    barrier = pltpu.get_barrier_semaphore()
    total = 0
    for dz in range(planes):
        for rel in range(4):
            for dr in range(2):
                if dz == 0 and rel == 0 and dr == 0:
                    continue
                pl.semaphore_signal(
                    barrier,
                    inc=1,
                    device_id={
                        "ctx": lax.rem(z + dz, planes),
                        "exp": at_xor(e, rel),
                        "rep": r if dr == 0 else 1 - r,
                    },
                    device_id_type=MESH,
                )
                total += 1
    pl.semaphore_wait(barrier, total)


LINKS = ("x", "y", "up", "down", "core")


def whole_wait(ref, sem):
    pltpu.make_async_copy(ref, ref, sem).wait()


def layer_kernel(
    planes, acts, grad, idx, prob, w_gate_in, w_up_in, w_down_in,
    acts_grad, gate_tok, gate_grad_out, up_grad_out, down_grad_out,
    acts_buf, grad_buf, gates, gates_all, gate_col,
    w_gate, w_up, w_down, gg_buf, gu_buf, gh_buf, gate_part, gate_in,
    terms_out, terms_own, core_buf, sum_buf, xy_buf, col_buf, z_buf,
    gate_grad, up_grad, down_grad,
    send_sem, recv_sem, swap_sem, gate_send, gate_recv, local_sem, weight_sem, result_sem,
    core_send, core_recv, xy_send, xy_recv, z_send, z_recv, g_send, g_recv,
):
    f32, bf16 = jnp.float32, jnp.bfloat16
    z, e, r = position()
    rows, width = acts.shape
    depth = 2 * width
    chips = planes * 4
    tokens = chips * rows
    plane_rows = 4 * rows
    top = idx.shape[0]
    hidden_here = w_gate.shape[0]

    loads = [
        pltpu.make_async_copy(src.at[0], dst, weight_sem.at[i])
        for i, (src, dst) in enumerate(((w_gate_in, w_gate), (w_up_in, w_up), (w_down_in, w_down)))
    ]
    for copy in loads:
        copy.start()
    idx_now, prob_now = idx[...], prob[...].astype(f32)
    for expert in range(chips):
        gates[expert, :, 0:rows] = jnp.sum(
            jnp.where(idx_now == expert, prob_now, 0.0), axis=0, keepdims=True
        )
        gates[expert, :, rows:LANES] = jnp.zeros((1, LANES - rows), f32)
    greet_all(planes)

    def others(with_core):
        for k in range(planes):
            for rel in range(4):
                for dr in range(2 if with_core else 1):
                    if k or rel or dr:
                        yield k, rel, dr

    def device(k, rel, dr):
        return {
            "ctx": lax.rem(z + k, planes),
            "exp": at_xor(e, rel),
            "rep": r if dr == 0 else 1 - r,
        }

    gate_copies = []
    for k, rel, _ in others(False):
        gate_copies.append(
            pltpu.make_async_remote_copy(
                src_ref=gates.at[lax.rem(z + k, planes) * 4 + at_xor(e, rel)],
                dst_ref=gates_all.at[z * 4 + rel],
                send_sem=gate_send.at[k, rel],
                recv_sem=gate_recv.at[k, rel],
                device_id=device(k, rel, 0),
                device_id_type=MESH,
            )
        )
    inputs, buffers = (acts, grad), (acts_buf, grad_buf)
    cols = pl.ds(pl.multiple_of(r * width, width), width)
    other_cols = pl.ds(pl.multiple_of((1 - r) * width, width), width)

    def chunk(array, source, rel, columns):
        return buffers[array].at[pl.ds((source * 4 + rel) * rows, rows), columns]

    mine = pl.ds(pl.multiple_of(z * plane_rows, plane_rows), rows)
    local = [
        pltpu.make_async_copy(inputs[a], buffers[a].at[mine, cols], local_sem.at[a]) for a in range(2)
    ]
    local.append(pltpu.make_async_copy(gates.at[z * 4 + e], gates_all.at[z * 4], local_sem.at[2]))

    def send(zi, array, source, rel, link, rel_there):
        target = {
            "x": {"ctx": z, "exp": at_xor(e, 1), "rep": r},
            "y": {"ctx": z, "exp": at_xor(e, 2), "rep": r},
            "up": {"ctx": z + 1, "exp": e, "rep": r},
            "down": {"ctx": z - 1, "exp": e, "rep": r},
            "core": {"ctx": z, "exp": e, "rep": 1 - r},
        }[link]
        own = source == zi and rel == 0
        sem = swap_sem if link == "core" else recv_sem
        return pltpu.make_async_remote_copy(
            src_ref=inputs[array] if own else chunk(array, source, rel, cols),
            dst_ref=chunk(array, source, rel_there, cols),
            send_sem=send_sem.at[LINKS.index(link), array, source, rel],
            recv_sem=sem.at[array, source, rel_there],
            device_id=target,
            device_id_type=MESH,
        )

    order = arrival_order(planes)
    for zi in range(planes):

        @pl.when(z == zi)
        def _():
            sent = []
            gates_out = False
            for array, source, rel in order[zi]:
                own = source == zi and rel == 0
                if not own:
                    if not gates_out:
                        for copy in gate_copies:
                            copy.start()
                        for copy in local:
                            copy.start()
                        gates_out = True
                    whole_wait(chunk(array, source, rel, cols), recv_sem.at[array, source, rel])
                steps = forwards(zi, planes, array, source, rel) + [("core", zi, rel)]
                for link, _, rel_there in steps:
                    copy = send(zi, array, source, rel, link, rel_there)
                    copy.start()
                    sent.append(copy)
            for copy in sent:
                copy.wait_send()

    for copy in local:
        copy.wait()
    for copy, (k, rel, _) in zip(gate_copies, others(False)):
        copy.wait_send()
        whole_wait(gates_all.at[lax.rem(z + planes - k, planes) * 4 + rel], gate_recv.at[k, rel])
    turned = jnp.transpose(jnp.concatenate([gates_all[s] for s in range(chips)], axis=0))
    for s in range(chips):
        gate_col[s * rows : (s + 1) * rows, :] = jnp.broadcast_to(turned[0:rows, s : s + 1], (rows, LANES))
    for copy in loads:
        copy.wait()
    for array in range(2):
        for source in range(planes):
            for rel in range(4):
                whole_wait(chunk(array, source, rel, other_cols), swap_sem.at[array, source, rel])

    partial = jnp.zeros((tokens, LANES), f32)
    for first in range(0, hidden_here, LANES):
        part = pl.ds(first, LANES)
        pre_gate = lax.dot_general(acts_buf[...], w_gate[part, :], CONTRACT_LAST, preferred_element_type=f32)
        pre_up = lax.dot_general(acts_buf[...], w_up[part, :], CONTRACT_LAST, preferred_element_type=f32)
        raw = lax.dot_general(grad_buf[...], w_down[part, :], CONTRACT_LAST, preferred_element_type=f32)
        sigma = jax.nn.sigmoid(pre_gate)
        swish = pre_gate * sigma
        hidden = (swish * pre_up).astype(bf16).astype(f32)
        partial = partial + hidden * raw
        hidden_grad = raw * gate_col[...]
        gg_buf[:, part] = (hidden_grad * pre_up * sigma * (1.0 + pre_gate * (1.0 - sigma))).astype(bf16)
        gu_buf[:, part] = (hidden_grad * swish).astype(bf16)
        gh_buf[:, part] = (hidden * gate_col[...]).astype(bf16)

    def terms(first, wide):
        part = pl.ds(pl.multiple_of(first, wide), wide)
        return jnp.dot(gg_buf[...], w_gate[:, part], preferred_element_type=f32) + jnp.dot(
            gu_buf[...], w_up[:, part], preferred_element_type=f32
        )

    wide = width // 2
    for first in range(0, width, wide):
        terms_out[:, pl.ds(first, wide)] = terms((1 - r) * width + first, wide).astype(bf16)
    after = list(range(1, planes)) + [0]
    core_copies = {}
    for k in after:
        place = pl.ds(pl.multiple_of(lax.rem(z + k, planes) * plane_rows, plane_rows), plane_rows)
        core_copies[k] = pltpu.make_async_remote_copy(
            src_ref=terms_out.at[place],
            dst_ref=core_buf.at[place],
            send_sem=core_send.at[k],
            recv_sem=core_recv.at[k],
            device_id=device(0, 0, 1),
            device_id_type=MESH,
        )
        core_copies[k].start()
    for first in range(0, width, wide):
        terms_own[:, pl.ds(first, wide)] = terms(r * width + first, wide)

    flat = jnp.sum(jnp.transpose(partial), axis=0, keepdims=True)
    for block in range(planes):
        gate_part[block] = flat[:, block * plane_rows : (block + 1) * plane_rows]

    xy_copies = {}
    for k in after:
        zz = lax.rem(z + k, planes)
        core_copies[k].wait_recv()
        for rel in (3, 1, 2, 0):
            block = pl.ds(pl.multiple_of((zz * 4 + rel) * rows, rows), rows)
            sum_buf[block, :] = (terms_own[block, :] + core_buf[block, :].astype(f32)).astype(bf16)
            if rel == 0:
                continue
            xy_copies[k, rel] = pltpu.make_async_remote_copy(
                src_ref=sum_buf.at[block],
                dst_ref=xy_buf.at[k, rel],
                send_sem=xy_send.at[k, rel],
                recv_sem=xy_recv.at[k, rel],
                device_id=device(0, rel, 0),
                device_id_type=MESH,
            )
            xy_copies[k, rel].start()
    part_copies = []
    slot = r * chips + z * 4
    for k, rel, dr in others(True):
        part_copies.append(
            pltpu.make_async_remote_copy(
                src_ref=gate_part.at[lax.rem(z + k, planes)],
                dst_ref=gate_in.at[slot + rel],
                send_sem=g_send.at[k, rel, dr],
                recv_sem=g_recv.at[k, rel, dr],
                device_id=device(k, rel, dr),
                device_id_type=MESH,
            )
        )
        part_copies[-1].start()
    own_part = pltpu.make_async_copy(gate_part.at[z], gate_in.at[slot], local_sem.at[3])
    own_part.start()

    def weight_grad(left, right, result, out, sem):
        for first in range(0, depth, 512):
            part = pl.ds(first, 512)
            result[:, part] = lax.dot_general(
                left[...], right[:, part], CONTRACT_FIRST, preferred_element_type=f32
            ).astype(bf16)
        copy = pltpu.make_async_copy(result, out.at[0], sem)
        copy.start()
        return copy

    results = [
        weight_grad(gg_buf, acts_buf, gate_grad, gate_grad_out, result_sem.at[0]),
        weight_grad(gu_buf, acts_buf, up_grad, up_grad_out, result_sem.at[1]),
    ]

    def column_total(k):
        block = pl.ds(pl.multiple_of((lax.rem(z + k, planes) * 4) * rows, rows), rows)
        total = sum_buf[block, :].astype(f32)
        for rel in (1, 2, 3):
            xy_copies[k, rel].wait_recv()
            total = total + xy_buf[k, rel].astype(f32)
        return total

    z_copies = {}
    for k in range(1, planes):
        col_buf[k] = column_total(k).astype(bf16)
        z_copies[k] = pltpu.make_async_remote_copy(
            src_ref=col_buf.at[k],
            dst_ref=z_buf.at[k],
            send_sem=z_send.at[k],
            recv_sem=z_recv.at[k],
            device_id=device(k, 0, 0),
            device_id_type=MESH,
        )
        z_copies[k].start()
    results.append(weight_grad(gh_buf, grad_buf, down_grad, down_grad_out, result_sem.at[2]))

    own_part.wait()
    for k, rel, dr in others(True):
        from_r = r if dr == 0 else 1 - r
        place = gate_in.at[from_r * chips + lax.rem(z + planes - k, planes) * 4 + rel]
        whole_wait(place, g_recv.at[k, rel, dr])
    token_grad = jnp.zeros((top, rows), f32)
    for s in range(chips):
        rel = s % 4
        row = (gate_in[s] + gate_in[chips + s]).astype(bf16).astype(f32)[:, rel * rows : (rel + 1) * rows]
        expert = (s // 4) * 4 + at_xor(e, rel)
        token_grad = token_grad + jnp.where(idx_now == expert, row, 0.0)
    gate_tok[...] = token_grad.astype(bf16)

    total = column_total(0)
    for k in range(1, planes):
        z_copies[k].wait_recv()
        total = total + z_buf[k].astype(f32)
    acts_grad[...] = total.astype(bf16)

    for copies in (core_copies, xy_copies, z_copies):
        for copy in copies.values():
            copy.wait_send()
    for copy in part_copies:
        copy.wait_send()
    for copy in results:
        copy.wait()


def dense_body(planes, acts, grad_out, experts_idx, gate_prob, w_gate, w_up, w_down):
    rows, width = acts.shape
    chips = planes * 4
    tokens = chips * rows
    depth = 2 * width
    hidden_here = w_gate.shape[1]
    dma = pltpu.SemaphoreType.DMA
    vmem, anywhere = pl.BlockSpec(memory_space=pltpu.VMEM), pl.BlockSpec(memory_space=pl.ANY)
    bf16, f32 = jnp.bfloat16, jnp.float32
    weight = pltpu.VMEM((hidden_here, depth), bf16)
    units = pltpu.VMEM((tokens, hidden_here), bf16)
    result = jax.ShapeDtypeStruct(w_gate.shape, bf16)
    block = (rows, width)

    acts_grad, gate_tok, gate_grad, up_grad, down_grad = pl.pallas_call(
        functools.partial(layer_kernel, planes),
        out_shape=(
            jax.ShapeDtypeStruct(block, bf16),
            jax.ShapeDtypeStruct(experts_idx.shape[::-1], bf16),
            result, result, result,
        ),
        in_specs=[vmem] * 4 + [anywhere] * 3,
        out_specs=[vmem] * 2 + [anywhere] * 3,
        scratch_shapes=[
            pltpu.VMEM((tokens, depth), bf16),
            pltpu.VMEM((tokens, depth), bf16),
            pltpu.VMEM((chips, 1, LANES), f32),
            pltpu.VMEM((chips, 1, LANES), f32),
            pltpu.VMEM((tokens, LANES), f32),
            weight, weight, weight,
            units, units, units,
            pltpu.VMEM((planes, 1, LANES), f32),
            pltpu.VMEM((2 * chips, 1, LANES), f32),
            pltpu.VMEM((tokens, width), bf16),
            pltpu.VMEM((tokens, width), f32),
            pltpu.VMEM((tokens, width), bf16),
            pltpu.VMEM((tokens, width), bf16),
            pltpu.VMEM((planes, 4, *block), bf16),
            pltpu.VMEM((planes, *block), bf16),
            pltpu.VMEM((planes, *block), bf16),
            weight, weight, weight,
            dma((len(LINKS), 2, planes, 4)),
            dma((2, planes, 4)),
            dma((2, planes, 4)),
            dma((planes, 4)),
            dma((planes, 4)),
            dma((4,)),
            dma((3,)),
            dma((3,)),
            dma((planes,)),
            dma((planes,)),
            dma((planes, 4)),
            dma((planes, 4)),
            dma((planes,)),
            dma((planes,)),
            dma((planes, 4, 2)),
            dma((planes, 4, 2)),
        ],
        compiler_params=pltpu.CompilerParams(
            collective_id=0, has_side_effects=True, vmem_limit_bytes=60 << 20
        ),
        name="layer",
    )(acts, grad_out, experts_idx.T, gate_prob.T, w_gate, w_up, w_down)
    return acts_grad, gate_tok.T, gate_grad, up_grad, down_grad


def body(planes, dense, acts, grad_out, experts_idx, *rest):
    run = functools.partial(dense_body, planes) if dense and 4 * acts.shape[0] == LANES else sparse_body
    return run(acts, grad_out, experts_idx, *rest)


def slot_tables(experts_idx, expert_count, capacity):
    tokens_here, top_count = experts_idx.shape
    labels = jnp.arange(expert_count, dtype=jnp.int32)
    picked = (experts_idx[:, :, None] == labels[None, None, :]).astype(jnp.int32)
    flat_pick = picked.reshape(tokens_here * top_count, expert_count)
    earlier = jnp.cumsum(flat_pick, axis=0) - flat_pick
    slot_number = jnp.sum(flat_pick * (labels[None, :] * capacity + earlier), axis=1)
    slot_labels = jnp.arange(expert_count * capacity, dtype=jnp.int32)
    select = (slot_number[None, :] == slot_labels[:, None]).astype(jnp.bfloat16)
    placing = jnp.sum(select.reshape(expert_count * capacity, tokens_here, top_count), axis=2)
    return (select, placing)


def sparse_body(acts, grad_out, experts_idx, gate_prob, w_gate, w_up, w_down):
    tokens_here, top_count = experts_idx.shape
    expert_count = lax.axis_size(("ctx", "exp"))
    capacity = min(tokens_here, 3 * tokens_here * top_count // (2 * expert_count))
    select, placing = slot_tables(experts_idx, expert_count, capacity)
    slot_gate = jnp.dot(select, gate_prob.reshape(-1), preferred_element_type=jnp.float32).astype(
        jnp.bfloat16
    )
    send_acts = jnp.dot(placing, acts, preferred_element_type=jnp.float32).astype(jnp.bfloat16)
    send_grad = jnp.dot(placing, grad_out, preferred_element_type=jnp.float32).astype(jnp.bfloat16)
    part_acts, part_grad, rows_gate = (
        lax.all_to_all(send_acts, ("ctx", "exp"), split_axis=0, concat_axis=0, tiled=True),
        lax.all_to_all(send_grad, ("ctx", "exp"), split_axis=0, concat_axis=0, tiled=True),
        lax.all_to_all(slot_gate, ("ctx", "exp"), split_axis=0, concat_axis=0, tiled=True),
    )
    rows_acts, rows_grad = (
        lax.all_gather(part_acts, "rep", axis=1, tiled=True),
        lax.all_gather(part_grad, "rep", axis=1, tiled=True),
    )
    gate_w = w_gate[0]
    up_w = w_up[0]
    down_w = w_down[0]
    contract_last = (((1,), (1,)), ((), ()))
    contract_first = (((0,), (0,)), ((), ()))
    pre_gate = lax.dot_general(rows_acts, gate_w, contract_last, preferred_element_type=jnp.float32)
    pre_up = lax.dot_general(rows_acts, up_w, contract_last, preferred_element_type=jnp.float32)
    sigma = jax.nn.sigmoid(pre_gate)
    swish = pre_gate * sigma
    hidden = (swish * pre_up).astype(jnp.bfloat16)
    expert_out = jnp.dot(hidden, down_w, preferred_element_type=jnp.float32)
    gate_part = jnp.sum(expert_out * rows_grad.astype(jnp.float32), axis=1)
    scaled_grad = (rows_gate.astype(jnp.float32)[:, None] * rows_grad.astype(jnp.float32)).astype(
        jnp.bfloat16
    )
    hidden_grad = lax.dot_general(
        scaled_grad, down_w, contract_last, preferred_element_type=jnp.float32
    )
    grad_gate_pre = (hidden_grad * pre_up * sigma * (1.0 + pre_gate * (1.0 - sigma))).astype(
        jnp.bfloat16
    )
    grad_up_pre = (hidden_grad * swish).astype(jnp.bfloat16)
    down_grad = lax.dot_general(
        hidden, scaled_grad, contract_first, preferred_element_type=jnp.float32
    ).astype(jnp.bfloat16)
    gate_grad = lax.dot_general(
        grad_gate_pre, rows_acts, contract_first, preferred_element_type=jnp.float32
    ).astype(jnp.bfloat16)
    up_grad = lax.dot_general(
        grad_up_pre, rows_acts, contract_first, preferred_element_type=jnp.float32
    ).astype(jnp.bfloat16)
    row_terms = jnp.dot(grad_gate_pre, gate_w, preferred_element_type=jnp.float32)
    row_terms = row_terms + jnp.dot(grad_up_pre, up_w, preferred_element_type=jnp.float32)
    row_share = lax.psum_scatter(
        row_terms.astype(jnp.bfloat16), "rep", scatter_dimension=1, tiled=True
    )
    gate_total = lax.psum(gate_part, "rep").astype(jnp.bfloat16)
    back_share, back_gate = (
        lax.all_to_all(row_share, ("ctx", "exp"), split_axis=0, concat_axis=0, tiled=True),
        lax.all_to_all(gate_total, ("ctx", "exp"), split_axis=0, concat_axis=0, tiled=True),
    )
    acts_grad = lax.dot_general(
        placing, back_share, contract_first, preferred_element_type=jnp.float32
    ).astype(jnp.bfloat16)
    gate_flat = lax.dot_general(
        select, back_gate, contract_first, preferred_element_type=jnp.float32
    )
    gate_grad_tok = gate_flat.reshape(tokens_here, top_count).astype(jnp.bfloat16)
    return (acts_grad, gate_grad_tok, gate_grad[None], up_grad[None], down_grad[None])


def solution(mesh):
    planes = mesh.shape["ctx"]
    dense = mesh.shape["exp"] == 4 and mesh.shape["rep"] == 2
    placed = (
        P(("ctx", "exp"), "rep"),
        P(("ctx", "exp"), "rep"),
        P(("ctx", "exp"), None),
        P(("ctx", "exp"), None),
        P(("ctx", "exp"), "rep", None),
        P(("ctx", "exp"), "rep", None),
        P(("ctx", "exp"), "rep", None),
    )
    return jax.shard_map(
        functools.partial(body, planes, dense),
        mesh=mesh,
        in_specs=placed,
        out_specs=(
            P(("ctx", "exp"), "rep"),
            P(("ctx", "exp"), None),
            P(("ctx", "exp"), "rep", None),
            P(("ctx", "exp"), "rep", None),
            P(("ctx", "exp"), "rep", None),
        ),
        check_vma=False,
    )
```

time: 82 us -> 65.5 us (0.80)
  Pallas kernels: 70.1 us -> 55.9 us
  other arithmetic: 2.09 us -> 0 us
    pallas_call x3 -> x1, Pallas kernels: 70.1 us -> 55.9 us  [dense_body(): pl.pallas_call(functools.partial(layer_kernel, planes), out_shape=(jax.Sh...]
    unnamed x11 -> x9, local copies, waits for them, and re-layouts: 6.27 us -> 8.68 us
    slice x2 -> x0, local copies, waits for them, and re-layouts: 1.44 us -> none  [the longest x1 0.72 us: dense_body(): gate_col = gates_all[:, 0, :rows].reshape(tokens, 1)]
    reduce_sum x2 -> x0, other arithmetic: 1.31 us -> none  [the longest x1 0.7 us: dense_body(): jnp.sum(jnp.where(picked, gate_prob.astype(f32).T[:, None, :], 0.0), axis=0)]
where the time goes in v2:
time: 65.5 us; the launch traced here: 65.2 us
  Pallas kernels  55.9 us (85%)
  local copies, waits for them, and re-layouts  8.68 us (13%)
    pallas_call x1, Pallas kernels, dense_body(): pl.pallas_call(functools.partial(layer_kernel, planes), out_shape=(jax.Sh...  55.9 us
    unnamed x9, local copies, waits for them, and re-layouts  8.68 us

profile of v2, /device:TPU:0, one launch (start us, length us, event | category | flops | bytes accessed | tf_op | source)
XLA Modules:
  0.0 65.2 jit_solution(13202220153002428345)
XLA Ops:
  0.6 55.9 %layer.1 = (bf16[32,1024]{1,0:T(8,128)(2,1)}, bf16[8,32]{1,0:T(8,128)(2,1)}, bf16[1,384,2048]{2,1,0:T(8,128)(2,1)}, bf16[1,384,2048]{2,1,0:T(8,128)(2,1)}, bf16[1,384,2048]{2,1,0:T(8,128)(2,1)}) custom-call(bf16[32,1024]{1,0:T(8,128)(2,1)} %acts.1, bf16[32,1024]{1,0:T(8,128)(2,1)} %grad.1, s32[8,32]{1,0:T(8,128)} %bitcast.3, bf16[8,32]{1,0:T(8,128)(2,1)} %bitcast.4, ...), custom_call_target="tpu_custom_call" | custom-call | tf_op jit(solution)/shard_map/layer/pallas_call | solution.py:398
  56.5 1.5 %copy.17 = bf16[32,1024]{1,0:T(8,128)(2,1)} copy(bf16[32,1024]{1,0:T(8,128)(2,1)} %get-tuple-element.20) | data formatting | bytes 131072
  58.0 1.2 %copy.18 = bf16[32,8]{0,1:T(8,128)(2,1)} copy(bf16[32,8]{0,1:T(8,128)(2,1)} %bitcast.5) | data formatting | bytes 1024
  59.3 0.0 copy-start.1
  59.3 2.8 %copy.19 = bf16[1,384,2048]{2,1,0:T(8,128)(2,1)} copy(bf16[1,384,2048]{2,1,0:T(8,128)(2,1)} %get-tuple-element.22) | data formatting | bytes 3145728
  62.1 0.0 copy-done.1
  62.1 0.0 copy-start
  62.1 1.1 %copy.20 = bf16[1,384,2048]{2,1,0:T(8,128)(2,1)} copy(bf16[1,384,2048]{2,1,0:T(8,128)(2,1)S(1)} %copy-done.1) | data formatting | bytes 3145728
  63.2 0.8 %copy-done = bf16[1,384,2048]{2,1,0:T(8,128)(2,1)S(1)} copy-done((bf16[1,384,2048]{2,1,0:T(8,128)(2,1)S(1)}, bf16[1,384,2048]{2,1,0:T(8,128)(2,1)}, u32[]{:S(2)}) %copy-start) | copy-done | bytes 1572888
  64.1 1.1 %copy.21 = bf16[1,384,2048]{2,1,0:T(8,128)(2,1)} copy(bf16[1,384,2048]{2,1,0:T(8,128)(2,1)S(1)} %copy-done) | data formatting | bytes 3145728
Async XLA Ops:
  59.3 2.9 %copy-start.1 = (bf16[1,384,2048]{2,1,0:T(8,128)(2,1)S(1)}, bf16[1,384,2048]{2,1,0:T(8,128)(2,1)}, u32[]{:S(2)}) copy-start(bf16[1,384,2048]{2,1,0:T(8,128)(2,1)} %get-tuple-element.23) | copy-start | bytes 4718596
  62.1 2.0 %copy-start = (bf16[1,384,2048]{2,1,0:T(8,128)(2,1)S(1)}, bf16[1,384,2048]{2,1,0:T(8,128)(2,1)}, u32[]{:S(2)}) copy-start(bf16[1,384,2048]{2,1,0:T(8,128)(2,1)} %get-tuple-element.24) | copy-start | bytes 4718596

commit v3 on v2

--- a/solution.py
+++ b/solution.py
@@ -106,9 +106,9 @@
 
 
 def layer_kernel(
-    planes, acts, grad, idx, prob, w_gate_in, w_up_in, w_down_in,
+    planes, acts, grad, idx_in, prob_in, w_gate_in, w_up_in, w_down_in,
     acts_grad, gate_tok, gate_grad_out, up_grad_out, down_grad_out,
-    acts_buf, grad_buf, gates, gates_all, gate_col,
+    acts_buf, grad_buf, idx, prob, gates, gates_all, gate_col,
     w_gate, w_up, w_down, gg_buf, gu_buf, gh_buf, gate_part, gate_in,
     terms_out, terms_own, core_buf, sum_buf, xy_buf, col_buf, z_buf,
     gate_grad, up_grad, down_grad,
@@ -125,18 +125,35 @@
     top = idx.shape[0]
     hidden_here = w_gate.shape[0]
 
+    buffers = (acts_buf, grad_buf)
+    cols = pl.ds(pl.multiple_of(r * width, width), width)
+    other_cols = pl.ds(pl.multiple_of((1 - r) * width, width), width)
+    mine = pl.ds(pl.multiple_of(z * plane_rows, plane_rows), rows)
+    local = [
+        pltpu.make_async_copy(src, dst, local_sem.at[i])
+        for i, (src, dst) in enumerate((
+            (idx_in, idx), (prob_in, prob),
+            (acts, acts_buf.at[mine, cols]), (grad, grad_buf.at[mine, cols]),
+        ))
+    ]
+    for copy in local:
+        copy.start()
     loads = [
         pltpu.make_async_copy(src.at[0], dst, weight_sem.at[i])
         for i, (src, dst) in enumerate(((w_gate_in, w_gate), (w_up_in, w_up), (w_down_in, w_down)))
     ]
     for copy in loads:
         copy.start()
+    for copy in local[:2]:
+        copy.wait()
     idx_now, prob_now = idx[...], prob[...].astype(f32)
     for expert in range(chips):
         gates[expert, :, 0:rows] = jnp.sum(
             jnp.where(idx_now == expert, prob_now, 0.0), axis=0, keepdims=True
         )
         gates[expert, :, rows:LANES] = jnp.zeros((1, LANES - rows), f32)
+    for copy in local[2:]:
+        copy.wait()
     greet_all(planes)
 
     def others(with_core):
@@ -165,18 +182,11 @@
                 device_id_type=MESH,
             )
         )
-    inputs, buffers = (acts, grad), (acts_buf, grad_buf)
-    cols = pl.ds(pl.multiple_of(r * width, width), width)
-    other_cols = pl.ds(pl.multiple_of((1 - r) * width, width), width)
 
     def chunk(array, source, rel, columns):
         return buffers[array].at[pl.ds((source * 4 + rel) * rows, rows), columns]
 
-    mine = pl.ds(pl.multiple_of(z * plane_rows, plane_rows), rows)
-    local = [
-        pltpu.make_async_copy(inputs[a], buffers[a].at[mine, cols], local_sem.at[a]) for a in range(2)
-    ]
-    local.append(pltpu.make_async_copy(gates.at[z * 4 + e], gates_all.at[z * 4], local_sem.at[2]))
+    own_gates = pltpu.make_async_copy(gates.at[z * 4 + e], gates_all.at[z * 4], local_sem.at[4])
 
     def send(zi, array, source, rel, link, rel_there):
         target = {
@@ -186,10 +196,9 @@
             "down": {"ctx": z - 1, "exp": e, "rep": r},
             "core": {"ctx": z, "exp": e, "rep": 1 - r},
         }[link]
-        own = source == zi and rel == 0
         sem = swap_sem if link == "core" else recv_sem
         return pltpu.make_async_remote_copy(
-            src_ref=inputs[array] if own else chunk(array, source, rel, cols),
+            src_ref=chunk(array, source, rel, cols),
             dst_ref=chunk(array, source, rel_there, cols),
             send_sem=send_sem.at[LINKS.index(link), array, source, rel],
             recv_sem=sem.at[array, source, rel_there],
@@ -210,8 +219,7 @@
                     if not gates_out:
                         for copy in gate_copies:
                             copy.start()
-                        for copy in local:
-                            copy.start()
+                        own_gates.start()
                         gates_out = True
                     whole_wait(chunk(array, source, rel, cols), recv_sem.at[array, source, rel])
                 steps = forwards(zi, planes, array, source, rel) + [("core", zi, rel)]
@@ -222,8 +230,7 @@
             for copy in sent:
                 copy.wait_send()
 
-    for copy in local:
-        copy.wait()
+    own_gates.wait()
     for copy, (k, rel, _) in zip(gate_copies, others(False)):
         copy.wait_send()
         whole_wait(gates_all.at[lax.rem(z + planes - k, planes) * 4 + rel], gate_recv.at[k, rel])
@@ -313,7 +320,7 @@
             )
         )
         part_copies[-1].start()
-    own_part = pltpu.make_async_copy(gate_part.at[z], gate_in.at[slot], local_sem.at[3])
+    own_part = pltpu.make_async_copy(gate_part.at[z], gate_in.at[slot], local_sem.at[5])
     own_part.start()
 
     def weight_grad(left, right, result, out, sem):
@@ -378,6 +385,16 @@
     for copy in part_copies:
         copy.wait_send()
     for copy in results:
+        copy.wait()
+
+
+def finish_kernel(*refs):
+    count = len(refs) // 2
+    sem = refs[-1]
+    copies = [pltpu.make_async_copy(refs[i], refs[count + i], sem.at[i]) for i in range(count)]
+    for copy in copies:
+        copy.start()
+    for copy in copies:
         copy.wait()
 
 
@@ -395,18 +412,21 @@
     result = jax.ShapeDtypeStruct(w_gate.shape, bf16)
     block = (rows, width)
 
-    acts_grad, gate_tok, gate_grad, up_grad, down_grad = pl.pallas_call(
+    shapes = (
+        jax.ShapeDtypeStruct(block, bf16),
+        jax.ShapeDtypeStruct(experts_idx.shape[::-1], bf16),
+        result, result, result,
+    )
+    results = pl.pallas_call(
         functools.partial(layer_kernel, planes),
-        out_shape=(
-            jax.ShapeDtypeStruct(block, bf16),
-            jax.ShapeDtypeStruct(experts_idx.shape[::-1], bf16),
-            result, result, result,
-        ),
-        in_specs=[vmem] * 4 + [anywhere] * 3,
+        out_shape=shapes,
+        in_specs=[pl.BlockSpec(memory_space=pltpu.HBM)] * 7,
         out_specs=[vmem] * 2 + [anywhere] * 3,
         scratch_shapes=[
             pltpu.VMEM((tokens, depth), bf16),
             pltpu.VMEM((tokens, depth), bf16),
+            pltpu.VMEM(experts_idx.shape[::-1], jnp.int32),
+            pltpu.VMEM(gate_prob.shape[::-1], bf16),
             pltpu.VMEM((chips, 1, LANES), f32),
             pltpu.VMEM((chips, 1, LANES), f32),
             pltpu.VMEM((tokens, LANES), f32),
@@ -427,7 +447,7 @@
             dma((2, planes, 4)),
             dma((planes, 4)),
             dma((planes, 4)),
-            dma((4,)),
+            dma((6,)),
             dma((3,)),
             dma((3,)),
             dma((planes,)),
@@ -440,10 +460,22 @@
             dma((planes, 4, 2)),
         ],
         compiler_params=pltpu.CompilerParams(
-            collective_id=0, has_side_effects=True, vmem_limit_bytes=60 << 20
+            collective_id=0, has_side_effects=True, vmem_limit_bytes=34 << 20
         ),
         name="layer",
-    )(acts, grad_out, experts_idx.T, gate_prob.T, w_gate, w_up, w_down)
+    )(*(
+        pltpu.with_memory_space_constraint(array, pltpu.HBM)
+        for array in (acts, grad_out, experts_idx.T, gate_prob.T, w_gate, w_up, w_down)
+    ))
+    acts_grad, gate_tok, gate_grad, up_grad, down_grad = pl.pallas_call(
+        finish_kernel,
+        out_shape=shapes,
+        in_specs=[vmem] * len(shapes),
+        out_specs=[anywhere] * len(shapes),
+        scratch_shapes=[dma((len(shapes),))],
+        compiler_params=pltpu.CompilerParams(vmem_limit_bytes=16 << 20),
+        name="finish",
+    )(*results)
     return acts_grad, gate_tok.T, gate_grad, up_grad, down_grad
 
 

time: 65.5 us -> 59.2 us (0.904)
  local copies, waits for them, and re-layouts: 8.68 us -> 0 us
  Pallas kernels: 55.9 us -> 58.4 us
    unnamed x9 -> x0, local copies, waits for them, and re-layouts: 8.68 us -> none
    pallas_call x1 -> x2, Pallas kernels: 55.9 us -> 58.4 us  [the longest x1 56.2 us: dense_body(): pl.pallas_call(functools.partial(layer_kernel, planes), out_shape=shapes,...]
where the time goes in v3:
time: 59.2 us; the launch traced here: 59.1 us
  Pallas kernels  58.4 us (99%)
  between operations  0.64 us (1%)
    pallas_call x1, Pallas kernels, dense_body(): pl.pallas_call(functools.partial(layer_kernel, planes), out_shape=shapes,...  56.2 us
    pallas_call x1, Pallas kernels, dense_body(): pl.pallas_call(finish_kernel, out_shape=shapes, in_specs=[vmem] * len(sha...  2.25 us

profile of v3, /device:TPU:0, one launch (start us, length us, event | category | flops | bytes accessed | tf_op | source)
XLA Modules:
  0.0 59.1 jit_solution(10586793453832455239)
XLA Ops:
  0.6 56.2 %layer.1 = (bf16[32,1024]{1,0:T(8,128)(2,1)S(1)}, bf16[8,32]{1,0:T(8,128)(2,1)S(1)}, bf16[1,384,2048]{2,1,0:T(8,128)(2,1)S(1)}, bf16[1,384,2048]{2,1,0:T(8,128)(2,1)S(1)}, bf16[1,384,2048]{2,1,0:T(8,128)(2,1)S(1)}) custom-call(bf16[32,1024]{1,0:T(8,128)(2,1)} %acts.1, bf16[32,1024]{1,0:T(8,128)(2,1)} %grad.1, s32[8,32]{1,0:T(8,128)} %bitcast.3, ...), custom_call_target="tpu_custom_call" | custom-call | tf_op jit(solution)/shard_map/layer/pallas_call | solution.py:420
  56.8 2.3 %finish.1 = (bf16[32,1024]{1,0:T(8,128)(2,1)}, bf16[8,32]{1,0:T(8,128)(2,1)}, bf16[1,384,2048]{2,1,0:T(8,128)(2,1)}, bf16[1,384,2048]{2,1,0:T(8,128)(2,1)}, bf16[1,384,2048]{2,1,0:T(8,128)(2,1)}) custom-call(bf16[32,1024]{1,0:T(8,128)(2,1)S(1)} %get-tuple-element.15.refs_0_, bf16[8,32]{1,0:T(8,128)(2,1)S(1)} %get-tuple-element.16.refs_1_, ...), custom_call_target="tpu_custom_call" | custom-call | tf_op jit(solution)/shard_map/finish/pallas_call | solution.py:470
